TPU v7x, 128 devices: a whole 4x4x4 slice. The times are simulated.
128 devices in a mesh: tm: 8 (over z, x_hi), docs: 16 (over y, x_lo, core).
Axes of the slice: x: 4 (x_hi: 2, x_lo: 2; x = x_hi * 2 + x_lo), y: 4, z: 4, core: 2. Of those that a mesh axis runs over, the one named last changes fastest.
Arguments:
- counts: int32 [8, 1024, 32768], P('tm', 'docs'), may hold values from 0 to 5, as said below
- topic_means: float32 [8, 32768, 128], P('tm', 'docs'), may hold values from -80 to 170
- doc_topics_init: float32 [8, 1024, 128], P('tm', 'docs'), may hold values from 0.5 to 20
- dirichlet_prior: float32 [128], replicated, may hold values from 0.05 to 1
- chain_var: float32 [128], replicated, may hold values from 0.005 to 0.5
- obs_noise: float32 [128], replicated, may hold values from 0.1 to 10
Outputs:
- smoothed_means: float32 [8, 32768, 128], P('tm', 'docs')
- doc_topics: float32 [8, 1024, 128], P('tm', 'docs')
Inputs may be any that keep to these rules, and one draw needn't show every extreme that they name: `counts`: each entry is 0 or a count of 1 to 5; each word has its own share of nonzero entries, between a quarter and three quarters.
All inputs are finite; a program needn't handle non-finite values.
Results may differ from a plain program's by a relative error of at most 0.01.
Values may be sent and summed in bfloat16 or wider, within the bound.
No kernel may reach another device: no remote copies, remote signals or barrier semaphores. Data moves between devices by JAX's collectives and lax.ppermute only.
A program may use at most 128 MiB of HBM per device.

v0:
```python
import jax
import jax.numpy as jnp
from jax import lax
from jax.sharding import Mesh
from jax.sharding import PartitionSpec as P

V = 32768
ITERS_E = 4
TM = ("tm_0", "tm_1")
TM_DOCS = ("tm_0", "tm_1", "docs")
prior_count = 0.5
initial_scale = 1000.0


def merged(part, axis, combine):
    gathered = jax.tree.map(lambda a: lax.all_gather(a, axis), part)

    def take(source):
        return jax.tree.map(lambda a: lax.dynamic_index_in_dim(a, source, 0, False), gathered)

    return lax.fori_loop(
        1, lax.axis_size(axis), lambda source, state: combine(state, take(source)), take(0)
    )


def filled_with(shard, identity):
    return jax.tree.map(
        lambda a, e: jnp.broadcast_to(jnp.asarray(e, a.dtype), a.shape), shard, identity
    )


def carried_in(shard, axes, combine, identity):
    before = start = filled_with(shard, identity)
    subtotal = shard
    for axis in reversed(axes):
        devices, place = (lax.axis_size(axis), lax.axis_index(axis))
        pieces = jax.tree.map(
            lambda part, kind: lax.all_gather(part.astype(kind), axis),
            subtotal,
            (jnp.bfloat16, jnp.bfloat16),
        )
        inside, subtotal = (start, start)
        for k in range(devices):
            passed = k < place
            subtotal = combine(
                subtotal, jax.tree.map(lambda part, own: part[k].astype(own.dtype), pieces, shard)
            )
            inside = jax.tree.map(lambda new, old: jnp.where(passed, new, old), subtotal, inside)
        before = combine(inside, before)
    return before


def prefix_by_axis(shard, axes, combine, identity):
    before = start = filled_with(shard, identity)
    subtotal = shard
    for axis in reversed(axes):
        devices, place = (lax.axis_size(axis), lax.axis_index(axis))
        pieces = jax.tree.map(
            lambda part, kind: lax.all_gather(part.astype(kind), axis),
            subtotal,
            jax.tree.map(lambda a: jnp.bfloat16 if a.dtype == jnp.float32 else a.dtype, shard),
        )
        inside, subtotal = (start, start)
        for k in reversed(range(devices)):
            passed = k > place
            subtotal = combine(
                subtotal, jax.tree.map(lambda part, own: part[k].astype(own.dtype), pieces, shard)
            )
            inside = jax.tree.map(lambda new, old: jnp.where(passed, new, old), subtotal, inside)
        before = combine(inside, before)
    return before


def chain_factors(totals, chain_var, obs_noise):
    relative = jnp.sum(totals, axis=1, keepdims=True) / (totals.shape[1] * totals)
    noise = obs_noise[None, :] * relative

    def advance(previous, noise_level):
        predicted = previous + chain_var
        own_gain = predicted / (predicted + noise_level)
        current = (1.0 - own_gain) * predicted
        return (current, (own_gain, current))

    unused, (gains, filtered_var) = lax.scan(advance, initial_scale * chain_var, noise)
    smooth = filtered_var / (filtered_var + chain_var)
    smooth = jnp.concatenate([smooth[:-1], jnp.zeros_like(smooth[-1:])], axis=0)
    return (gains, smooth)


def compose(former, latter):
    return (former[0] * latter[0], latter[0] * former[1] + latter[1])


def join_mass(former, latter):
    highest = jnp.maximum(former[0], latter[0])
    return (
        highest,
        former[1] * jnp.exp(former[0] - highest) + latter[1] * jnp.exp(latter[0] - highest),
    )


def body(counts, topic_means, doc_topics_init, dirichlet_prior, chain_var, obs_noise):
    topic_slab = topic_means[0]
    concentration = doc_topics_init[0]
    count_wide = counts[0].astype(jnp.float32)
    local_peak = jnp.max(topic_slab, axis=0)
    local_mass = jnp.sum(jnp.exp(topic_slab - local_peak[None, :]), axis=0)
    column_peak, column_mass = merged((local_peak, local_mass), "docs", join_mass)
    beta_slab = jnp.exp(topic_slab - (column_peak + jnp.log(column_mass))[None, :]).astype(
        jnp.bfloat16
    )
    beta_full = lax.all_gather(beta_slab, "docs", axis=0, tiled=True)
    for sweep_index in range(ITERS_E):
        proportions = jnp.exp(lax.digamma(concentration)).astype(jnp.bfloat16)
        mixture = lax.dot_general(
            proportions, beta_full, (((1,), (1,)), ((), ())), preferred_element_type=jnp.float32
        )
        ratios = (count_wide / mixture).astype(jnp.bfloat16)
        update = proportions.astype(jnp.float32) * jnp.dot(
            ratios, beta_full, preferred_element_type=jnp.float32
        )
        concentration = dirichlet_prior[None, :] + update
    word_stats = lax.psum_scatter(
        (
            beta_full.astype(jnp.float32)
            * lax.dot_general(
                ratios, proportions, (((0,), (0,)), ((), ())), preferred_element_type=jnp.float32
            )
        ).astype(jnp.bfloat16),
        "docs",
        scatter_dimension=0,
        tiled=True,
    ).astype(jnp.float32)
    slice_index = lax.axis_index(TM)
    slices = lax.axis_size(TM)
    own_row = (jnp.arange(slices) == slice_index).astype(jnp.float32)
    placed = own_row[:, None] * jnp.sum(update, axis=0)[None, :]
    totals = lax.psum(placed, TM_DOCS)
    gains, smooth = chain_factors(totals, chain_var, obs_noise)
    own_total = jnp.sum(own_row[:, None] * totals, axis=0)
    own_gain = jnp.sum(own_row[:, None] * gains, axis=0)
    own_factor = jnp.sum(own_row[:, None] * smooth, axis=0)
    pseudo = jnp.log(word_stats + prior_count) - jnp.log((own_total + prior_count * V) / V)[None, :]
    forward_rate = 1.0 - own_gain
    forward_term = own_gain[None, :] * pseudo
    neutral = (jnp.ones_like(forward_rate), jnp.zeros_like(forward_term))
    entering = carried_in((forward_rate, forward_term), TM, compose, neutral)[1]
    filtered = forward_rate[None, :] * entering + forward_term
    back_term = (1.0 - own_factor)[None, :] * filtered
    following = prefix_by_axis((own_factor, back_term), TM, compose, neutral)[1]
    smoothed = own_factor[None, :] * following + back_term
    return (smoothed[None], concentration[None])


def solution(mesh):
    split = Mesh(mesh.devices.reshape(4, 2, mesh.shape["docs"]), ("tm_0", "tm_1", "docs"))
    placed = (P(TM, "docs", None), P(TM, "docs", None), P(TM, "docs", None), P(), P(), P())
    return jax.shard_map(
        body,
        mesh=split,
        in_specs=placed,
        out_specs=(P(TM, "docs", None), P(TM, "docs", None)),
        check_vma=False,
    )
```

profile of v0, /device:TPU:1, one launch (start us, length us, event | category | flops | bytes accessed | tf_op | source)
XLA Modules:
  0.0 390.9 jit_solution(17476896300496999206)
XLA Ops:
  10.2 21.2 %all-gather.7 = f32[16,1,128]{2,1,0:T(1,128)S(1)} all-gather(f32[1,1,128]{2,1,0:T(1,128)S(1)} %bitcast.319), channel_id=3, replica_groups=mesh['tm_0'=4,'tm_1'=2,'docs'=16] {'docs'}, dimensions={0}, use_global_device_ids=true | all-gather | bytes 8704 | tf_op jit(solution)/shard_map/all_gather | solution.py:16
  31.4 16.3 %all-gather.6 = f32[16,1,128]{2,1,0:T(1,128)S(1)} all-gather(f32[1,1,128]{2,1,0:T(1,128)S(1)} %bitcast.318), channel_id=2, replica_groups=mesh['tm_0'=4,'tm_1'=2,'docs'=16] {'docs'}, dimensions={0}, use_global_device_ids=true | all-gather | bytes 8704 | tf_op jit(solution)/shard_map/all_gather | solution.py:16
  48.4 2.2 fusion.53
  50.6 51.7 %all-gather.18.cloned.1.call-done = bf16[32768,128]{1,0:T(8,128)(2,1)} async-done(((bf16[2048,128]{1,0:T(8,128)(2,1)}), bf16[32768,128]{1,0:T(8,128)(2,1)}) %all-gather.18.cloned.1.call-update) | async-done | bytes 8388624 | tf_op jit(solution)/shard_map/all_gather | solution.py:112
  102.3 13.1 %fusion.62 = bf16[64,128]{1,0:T(8,128)(2,1)S(1)} fusion(bf16[32768,128]{1,0:T(8,128)(2,1)} %all-gather.18.cloned.1.call-done, s32[1,64,32768]{2,1,0:T(8,128)} %param.10, f32[1,64,128]{2,1,0:T(8,128)} %param.12, f32[128]{0:T(128)} %param.13), kind=kOutput, calls=%fused_computation.109 | convolution fusion | flops 1081925632 | bytes 16826880 | tf_op jit(solution)/shard_map/dot_general | solution.py:119
  115.4 12.6 %fusion.66 = bf16[64,128]{1,0:T(8,128)(2,1)S(1)} fusion(bf16[32768,128]{1,0:T(8,128)(2,1)} %all-gather.18.cloned.1.call-done, bf16[64,128]{1,0:T(8,128)(2,1)S(1)} %fusion.62, s32[1,64,32768]{2,1,0:T(8,128)} %param.10, f32[128]{0:T(128)S(1)} %copy-done.2), kind=kOutput, calls=%fused_computation.113 | convolution fusion | flops 1080680448 | bytes 16810496 | tf_op jit(solution)/shard_map/dot_general | solution.py:119
  128.0 12.4 %fusion.15 = f32[64,128]{1,0:T(8,128)S(1)} fusion(bf16[32768,128]{1,0:T(8,128)(2,1)} %all-gather.18.cloned.1.call-done, bf16[64,128]{1,0:T(8,128)(2,1)S(1)} %fusion.66, s32[1,64,32768]{2,1,0:T(8,128)} %param.10, f32[128]{0:T(128)S(1)} %copy-done.2), kind=kOutput, calls=%fused_computation.35 | convolution fusion | flops 1080057856 | bytes 16826880 | tf_op jit(solution)/shard_map/dot_general | solution.py:119
  140.4 9.2 %fusion.3 = bf16[64,32768]{1,0:T(8,128)(2,1)S(1)} fusion(bf16[32768,128]{1,0:T(8,128)(2,1)} %all-gather.18.cloned.1.call-done, s32[1,64,32768]{2,1,0:T(8,128)} %param.10, f32[64,128]{1,0:T(8,128)S(1)} %fusion.15), kind=kOutput, calls=%fused_computation.11 | convolution fusion | flops 543784960 | bytes 21004288 | tf_op jit(solution)/shard_map/dot_general | solution.py:115
  151.5 7.3 %fusion.2 = bf16[32768,128]{1,0:T(8,128)(2,1)} fusion(bf16[64,32768]{1,0:T(8,128)(2,1)S(1)} %fusion.3, bf16[32768,128]{1,0:T(8,128)(2,1)} %all-gather.18.cloned.1.call-done, f32[64,128]{1,0:T(8,128)S(1)} %fusion.15), kind=kOutput, calls=%fused_computation.9 | convolution fusion | flops 550076416 | bytes 21004288 | tf_op jit(solution)/shard_map/dot_general | solution.py:126
  159.5 7.0 %add_bitcast_fusion = (f32[1,64,128]{2,1,0:T(8,128)}, f32[128]{0:T(128)S(1)}) fusion(f32[128]{0:T(128)S(1)} %copy-done.2, bf16[64,32768]{1,0:T(8,128)(2,1)} %copy-done, bf16[32768,128]{1,0:T(8,128)(2,1)} %all-gather.18.cloned.1.call-done, f32[64,128]{1,0:T(8,128)S(1)} %fusion.15), kind=kOutput, calls=%fused_computation.129 | convolution fusion | flops 537526144 | bytes 12649472 | tf_op jit(solution)/shard_map/dot_general | solution.py:119
  166.6 67.0 %psum.7 = f32[8,128]{1,0:T(8,128)S(1)} all-reduce(f32[8,128]{1,0:T(8,128)S(1)} %broadcast_multiply_fusion), channel_id=1, replica_groups=mesh['tm_0'=4,'tm_1'=2,'docs'=16] {'tm_0','tm_1','docs'}, use_global_device_ids=true, to_apply=%region_5.6 | all-reduce | flops 1024 | bytes 8192 | tf_op jit(solution)/shard_map/psum | solution.py:138
  234.8 22.3 %reduce-scatter.2.cloned.1.call-done = bf16[2048,128]{1,0:T(8,128)(2,1)} async-done(((bf16[32768,128]{1,0:T(8,128)(2,1)}), bf16[2048,128]{1,0:T(8,128)(2,1)}) %reduce-scatter.2.cloned.1.call-update) | async-done | bytes 524304 | tf_op jit(solution)/shard_map/reduce_scatter | solution.py:123
  259.3 4.6 %all-gather.10 = bf16[2,1,128]{2,1,0:T(2,128)(2,1)S(1)} all-gather(bf16[1,1,128]{2,1,0:T(2,128)(2,1)S(1)} %get-tuple-element.221), channel_id=5, replica_groups=mesh['tm_0'=4,'tm_1'=2,'docs'=16] {'tm_1'}, dimensions={0}, use_global_device_ids=true | all-gather | bytes 768 | tf_op jit(solution)/shard_map/all_gather | solution.py:38
  263.9 21.5 %all-gather.24.cloned.1.call-done = bf16[4096,128]{1,0:T(8,128)(2,1)} async-done(((bf16[2048,128]{1,0:T(8,128)(2,1)}), bf16[4096,128]{1,0:T(8,128)(2,1)}) %all-gather.24.cloned.1.call-update) | async-done | bytes 1048592 | tf_op jit(solution)/shard_map/all_gather | solution.py:38
  285.4 2.2 fusion.33
  287.7 7.9 %all-gather.11 = bf16[4,1,128]{2,1,0:T(2,128)(2,1)S(1)} all-gather(bf16[1,1,128]{2,1,0:T(2,128)(2,1)S(1)} %get-tuple-element.216), channel_id=1, replica_groups=mesh['tm_0'=4,'tm_1'=2,'docs'=16] {'tm_0'}, dimensions={0}, use_global_device_ids=true | all-gather | bytes 1280 | tf_op jit(solution)/shard_map/all_gather | solution.py:38
  295.6 22.6 %all-gather.20.cloned.1.call-done = bf16[4,2048,128]{2,1,0:T(8,128)(2,1)} async-done(((bf16[1,2048,128]{2,1,0:T(8,128)(2,1)}), bf16[4,2048,128]{2,1,0:T(8,128)(2,1)}) %all-gather.20.cloned.1.call-update) | async-done | bytes 2097168 | tf_op jit(solution)/shard_map/all_gather | solution.py:38
  318.2 3.9 %fusion.309 = (bf16[2048,128]{1,0:T(8,128)(2,1)}, f32[2048,128]{1,0:T(8,128)S(1)}) fusion(f32[128]{0:T(128)S(1)} %multiply_log_fusion, bf16[2048,128]{1,0:T(8,128)(2,1)} %reduce-scatter.2.cloned.1.call-done, f32[128]{0:T(128)S(1)} %get-tuple-element.175, pred[]{:T(512)S(6)} %gt.19, bf16[4096,128]{1,0:T(8,128)(2,1)} %all-gather.24.cloned.1.call-done, ...), kind=kLoop, calls=%fused_computation.345 | loop fusion | flops 8388608 | bytes 5248518 | tf_op jit(solution)/shard_map/convert_element_type | solution.py:59
  322.2 4.6 %all-gather.8 = bf16[2,1,128]{2,1,0:T(2,128)(2,1)S(1)} all-gather(bf16[1,1,128]{2,1,0:T(2,128)(2,1)S(1)} %get-tuple-element.218), channel_id=4, replica_groups=mesh['tm_0'=4,'tm_1'=2,'docs'=16] {'tm_1'}, dimensions={0}, use_global_device_ids=true | all-gather | bytes 768 | tf_op jit(solution)/shard_map/all_gather | solution.py:59
  326.8 20.7 %all-gather.26.cloned.1.call-done = bf16[4096,128]{1,0:T(8,128)(2,1)} async-done(((bf16[2048,128]{1,0:T(8,128)(2,1)}), bf16[4096,128]{1,0:T(8,128)(2,1)}) %all-gather.26.cloned.1.call-update) | async-done | bytes 1048592 | tf_op jit(solution)/shard_map/all_gather | solution.py:59
  347.5 2.2 fusion.37
  349.7 7.9 %all-gather.9 = bf16[4,1,128]{2,1,0:T(2,128)(2,1)S(1)} all-gather(bf16[1,1,128]{2,1,0:T(2,128)(2,1)S(1)} %get-tuple-element.212), channel_id=1, replica_groups=mesh['tm_0'=4,'tm_1'=2,'docs'=16] {'tm_0'}, dimensions={0}, use_global_device_ids=true | all-gather | bytes 1280 | tf_op jit(solution)/shard_map/all_gather | solution.py:59
  357.6 22.7 %all-gather.22.cloned.1.call-done = bf16[4,2048,128]{2,1,0:T(8,128)(2,1)} async-done(((bf16[1,2048,128]{2,1,0:T(8,128)(2,1)}), bf16[4,2048,128]{2,1,0:T(8,128)(2,1)}) %all-gather.22.cloned.1.call-update) | async-done | bytes 2097168 | tf_op jit(solution)/shard_map/all_gather | solution.py:59
  380.3 3.7 fusion.24
  (88 shorter events, 11.0 us)
Async XLA Ops:
  7.2 95.1 %all-gather.18.cloned.1.call-start = ((), (), s32[]{:S(2)}) async-start(), calls=%async_computation.1 | async-start | bytes 8912896 | tf_op jit(solution)/shard_map/all_gather | solution.py:112
  50.6 64.9 %copy-start.2 = (f32[128]{0:T(128)S(1)}, f32[128]{0:T(128)}, u32[]{:S(2)}) copy-start(f32[128]{0:T(128)} %param.13) | copy-start | bytes 1540
  50.6 206.5 %reduce-scatter.2.cloned.1.call-start = ((), (), s32[]{:S(2)}) async-start(), calls=%async_computation.2 | async-start | bytes 8912896 | tf_op jit(solution)/shard_map/reduce_scatter | solution.py:123
  149.6 1.9 copy-start
  158.8 0.7 copy-start.1
  158.9 126.5 %all-gather.24.cloned.1.call-start = ((), (), s32[]{:S(2)}) async-start(), calls=%async_computation.5 | async-start | bytes 1572864 | tf_op jit(solution)/shard_map/all_gather | solution.py:38
  159.5 74.2 %copy-start.3 = (f32[128]{0:T(128)S(1)}, f32[128]{0:T(128)}, u32[]{:S(2)}) copy-start(f32[128]{0:T(128)} %param.15) | copy-start | bytes 1540
  159.5 75.2 %copy-start.4 = (pred[8]{0:T(512)(128)(4,1)S(1)}, pred[8]{0:T(512)(128)(4,1)}, u32[]{:S(2)}) copy-start(pred[8]{0:T(512)(128)(4,1)} %constant.117.clone.1) | copy-start | bytes 28
  259.2 59.0 %all-gather.20.cloned.1.call-start = ((), (), s32[]{:S(2)}) async-start(), calls=%async_computation.3 | async-start | bytes 2621440 | tf_op jit(solution)/shard_map/all_gather | solution.py:38
  287.6 59.9 %all-gather.26.cloned.1.call-start = ((), (), s32[]{:S(2)}) async-start(), calls=%async_computation.6 | async-start | bytes 1572864 | tf_op jit(solution)/shard_map/all_gather | solution.py:59
  322.2 58.1 %all-gather.22.cloned.1.call-start = ((), (), s32[]{:S(2)}) async-start(), calls=%async_computation.4 | async-start | bytes 2621440 | tf_op jit(solution)/shard_map/all_gather | solution.py:59
Sparse Core Ops, SparseCore 0:
  50.7 51.5 all-gather.17
  159.0 98.0 reduce-scatter.1
  259.3 26.0 all-gather.23
  287.7 30.4 all-gather.19
  322.3 25.1 all-gather.25
  349.8 30.4 all-gather.21
where the time goes:
time: 391 us
  waiting for transfers between devices  162 us (41%)
  blocking collectives  129 us (33%)
  matrix products  61.6 us (16%)
  other arithmetic  20.3 us (5%)
  between operations  14.3 us (4%)
    psum x1, blocking collectives, body(): totals = lax.psum(placed, TM_DOCS)  67 us
    all_gather x1, waiting for transfers between devices, body(): beta_full = lax.all_gather(beta_slab, 'docs', axis=0, tiled=True)  51.7 us
    dot_general x4, matrix products, body(): jnp.dot(ratios, beta_full, preferred_element_type=jnp.float32)  45.1 us
    all_gather x2, waiting for transfers between devices, carried_in(): lax.all_gather(part.astype(kind), axis)  44.2 us
    all_gather x2, waiting for transfers between devices, prefix_by_axis(): lax.all_gather(part.astype(kind), axis)  43.4 us
    all_gather x2, blocking collectives, merged(): gathered = jax.tree.map(lambda a: lax.all_gather(a, axis), part)  37.5 us
    reduce_scatter x1, waiting for transfers between devices, body(): lax.psum_scatter((beta_full.astype(jnp.float32) * lax.dot_general(ratios,...  22.3 us
    all_gather x2, blocking collectives, carried_in(): lax.all_gather(part.astype(kind), axis)  12.5 us
  transfers between devices with their start and end apart: 6, of which 6 were waited for; matrix products, arithmetic and copies ran while one was open for 2% of the time, Pallas kernels for 0%

commit v1 on v0

--- a/solution.py
+++ b/solution.py
@@ -109,7 +109,8 @@
     beta_slab = jnp.exp(topic_slab - (column_peak + jnp.log(column_mass))[None, :]).astype(
         jnp.bfloat16
     )
-    beta_full = lax.all_gather(beta_slab, "docs", axis=0, tiled=True)
+    sent = jnp.stack([beta_slab] * lax.axis_size("docs"))
+    beta_full = jnp.concatenate(lax.all_to_all(sent, "docs", 0, 0), axis=0)
     for sweep_index in range(ITERS_E):
         proportions = jnp.exp(lax.digamma(concentration)).astype(jnp.bfloat16)
         mixture = lax.dot_general(

time: 391 us -> 437 us (1.12)
  blocking collectives: 129 us -> 227 us
  waiting for transfers between devices: 162 us -> 110 us
    all_to_all x0 -> x1, blocking collectives: none -> 97.5 us  [body(): beta_full = jnp.concatenate(lax.all_to_all(sent, 'docs', 0, 0), axis=0)]
    all_gather x1 -> x0, waiting for transfers between devices: 51.7 us -> none  [body(): beta_full = lax.all_gather(beta_slab, 'docs', axis=0, tiled=True)]
  transfers between devices with their start and end apart: 6 -> 5, of which waited for: 6 -> 5; matrix products, arithmetic and copies ran while one was open for 2% -> 2% of each run, Pallas kernels for 0% -> 0%
where the time goes in v1:
time: 437 us
  blocking collectives  227 us (52%)
  waiting for transfers between devices  110 us (25%)
  matrix products  61.6 us (14%)
  other arithmetic  19.5 us (4%)
  between operations  14 us (3%)
  local copies, waits for them, and re-layouts  4.66 us (1%)
    all_to_all x1, blocking collectives, body(): beta_full = jnp.concatenate(lax.all_to_all(sent, 'docs', 0, 0), axis=0)  97.5 us
    psum x1, blocking collectives, body(): totals = lax.psum(placed, TM_DOCS)  66.8 us
    dot_general x4, matrix products, body(): jnp.dot(ratios, beta_full, preferred_element_type=jnp.float32)  45.1 us
    all_gather x2, waiting for transfers between devices, carried_in(): lax.all_gather(part.astype(kind), axis)  44.1 us
    all_gather x2, waiting for transfers between devices, prefix_by_axis(): lax.all_gather(part.astype(kind), axis)  43.4 us
    all_gather x2, blocking collectives, merged(): gathered = jax.tree.map(lambda a: lax.all_gather(a, axis), part)  37.5 us
    reduce_scatter x1, waiting for transfers between devices, body(): lax.psum_scatter((beta_full.astype(jnp.float32) * lax.dot_general(ratios,...  22.2 us
    all_gather x2, blocking collectives, carried_in(): lax.all_gather(part.astype(kind), axis)  12.5 us
  transfers between devices with their start and end apart: 5, of which 5 were waited for; matrix products, arithmetic and copies ran while one was open for 2% of the time, Pallas kernels for 0%

profile of v1, /device:TPU:1, one launch (start us, length us, event | category | flops | bytes accessed | tf_op | source)
XLA Modules:
  0.0 436.9 jit_solution(6214261179668147207)
XLA Ops:
  10.2 21.2 %all-gather.7 = f32[16,1,128]{2,1,0:T(1,128)S(1)} all-gather(f32[1,1,128]{2,1,0:T(1,128)S(1)} %bitcast.324), channel_id=3, replica_groups=mesh['tm_0'=4,'tm_1'=2,'docs'=16] {'docs'}, dimensions={0}, use_global_device_ids=true | all-gather | bytes 8704 | tf_op jit(solution)/shard_map/all_gather | solution.py:16
  31.4 16.3 %all-gather.6 = f32[16,1,128]{2,1,0:T(1,128)S(1)} all-gather(f32[1,1,128]{2,1,0:T(1,128)S(1)} %bitcast.323), channel_id=2, replica_groups=mesh['tm_0'=4,'tm_1'=2,'docs'=16] {'docs'}, dimensions={0}, use_global_device_ids=true | all-gather | bytes 8704 | tf_op jit(solution)/shard_map/all_gather | solution.py:16
  51.4 97.5 %all_to_all.5 = bf16[16,2048,128]{2,1,0:T(8,128)(2,1)} all-to-all(bf16[16,2048,128]{2,1,0:T(8,128)(2,1)S(1)} %stack.5), channel_id=1, replica_groups=mesh['tm_0'=4,'tm_1'=2,'docs'=16] {'docs'}, dimensions={0} | all-to-all | bytes 16777216 | tf_op jit(solution)/shard_map/all_to_all | solution.py:113
  148.9 13.1 %fusion.65 = bf16[64,128]{1,0:T(8,128)(2,1)S(1)} fusion(bf16[32768,128]{1,0:T(8,128)(2,1)} %bitcast.313, s32[1,64,32768]{2,1,0:T(8,128)} %param.10, f32[1,64,128]{2,1,0:T(8,128)S(1)} %copy-done.5, f32[128]{0:T(128)S(1)} %copy-done.2), kind=kOutput, calls=%fused_computation.114 | convolution fusion | flops 1081925632 | bytes 16826880 | tf_op jit(solution)/shard_map/dot_general | solution.py:120
  162.0 12.6 %fusion.69 = bf16[64,128]{1,0:T(8,128)(2,1)S(1)} fusion(bf16[32768,128]{1,0:T(8,128)(2,1)} %bitcast.314, bf16[64,128]{1,0:T(8,128)(2,1)S(1)} %fusion.65, s32[1,64,32768]{2,1,0:T(8,128)} %param.10, f32[128]{0:T(128)S(1)} %copy-done.2), kind=kOutput, calls=%fused_computation.118 | convolution fusion | flops 1080680448 | bytes 16810496 | tf_op jit(solution)/shard_map/dot_general | solution.py:120
  174.6 12.4 %fusion.15 = f32[64,128]{1,0:T(8,128)S(1)} fusion(bf16[32768,128]{1,0:T(8,128)(2,1)} %bitcast.315, bf16[64,128]{1,0:T(8,128)(2,1)S(1)} %fusion.69, s32[1,64,32768]{2,1,0:T(8,128)} %param.10, f32[128]{0:T(128)S(1)} %copy-done.2), kind=kOutput, calls=%fused_computation.35 | convolution fusion | flops 1080057856 | bytes 16826880 | tf_op jit(solution)/shard_map/dot_general | solution.py:120
  186.9 9.2 %fusion.3 = bf16[64,32768]{1,0:T(8,128)(2,1)S(1)} fusion(bf16[32768,128]{1,0:T(8,128)(2,1)} %bitcast.316, s32[1,64,32768]{2,1,0:T(8,128)} %param.10, f32[64,128]{1,0:T(8,128)S(1)} %fusion.15), kind=kOutput, calls=%fused_computation.11 | convolution fusion | flops 543784960 | bytes 21004288 | tf_op jit(solution)/shard_map/dot_general | solution.py:116
  198.1 7.3 %fusion.2 = bf16[32768,128]{1,0:T(8,128)(2,1)} fusion(bf16[64,32768]{1,0:T(8,128)(2,1)S(1)} %fusion.3, bf16[32768,128]{1,0:T(8,128)(2,1)} %bitcast.317, f32[64,128]{1,0:T(8,128)S(1)} %fusion.15), kind=kOutput, calls=%fused_computation.9 | convolution fusion | flops 550076416 | bytes 21004288 | tf_op jit(solution)/shard_map/dot_general | solution.py:127
  206.1 7.0 %add_bitcast_fusion = (f32[1,64,128]{2,1,0:T(8,128)}, f32[128]{0:T(128)S(1)}) fusion(f32[128]{0:T(128)S(1)} %copy-done.2, bf16[64,32768]{1,0:T(8,128)(2,1)} %copy-done, bf16[32768,128]{1,0:T(8,128)(2,1)} %bitcast.318, f32[64,128]{1,0:T(8,128)S(1)} %fusion.15), kind=kOutput, calls=%fused_computation.134 | convolution fusion | flops 537526144 | bytes 12649472 | tf_op jit(solution)/shard_map/dot_general | solution.py:120
  213.2 66.8 %psum.7 = f32[8,128]{1,0:T(8,128)S(1)} all-reduce(f32[8,128]{1,0:T(8,128)S(1)} %broadcast_multiply_fusion), channel_id=1, replica_groups=mesh['tm_0'=4,'tm_1'=2,'docs'=16] {'tm_0','tm_1','docs'}, use_global_device_ids=true, to_apply=%region_5.6 | all-reduce | flops 1024 | bytes 8192 | tf_op jit(solution)/shard_map/psum | solution.py:139
  281.2 22.2 %reduce-scatter.2.cloned.1.call-done = bf16[2048,128]{1,0:T(8,128)(2,1)} async-done(((bf16[32768,128]{1,0:T(8,128)(2,1)}), bf16[2048,128]{1,0:T(8,128)(2,1)}) %reduce-scatter.2.cloned.1.call-update) | async-done | bytes 524304 | tf_op jit(solution)/shard_map/reduce_scatter | solution.py:124
  303.4 2.1 fusion.52
  305.6 4.6 %all-gather.10 = bf16[2,1,128]{2,1,0:T(2,128)(2,1)S(1)} all-gather(bf16[1,1,128]{2,1,0:T(2,128)(2,1)S(1)} %get-tuple-element.221), channel_id=5, replica_groups=mesh['tm_0'=4,'tm_1'=2,'docs'=16] {'tm_1'}, dimensions={0}, use_global_device_ids=true | all-gather | bytes 768 | tf_op jit(solution)/shard_map/all_gather | solution.py:38
  310.2 21.5 %all-gather.21.cloned.1.call-done = bf16[4096,128]{1,0:T(8,128)(2,1)} async-done(((bf16[2048,128]{1,0:T(8,128)(2,1)}), bf16[4096,128]{1,0:T(8,128)(2,1)}) %all-gather.21.cloned.1.call-update) | async-done | bytes 1048592 | tf_op jit(solution)/shard_map/all_gather | solution.py:38
  331.7 2.2 fusion.33
  334.0 7.9 %all-gather.11 = bf16[4,1,128]{2,1,0:T(2,128)(2,1)S(1)} all-gather(bf16[1,1,128]{2,1,0:T(2,128)(2,1)S(1)} %get-tuple-element.216), channel_id=1, replica_groups=mesh['tm_0'=4,'tm_1'=2,'docs'=16] {'tm_0'}, dimensions={0}, use_global_device_ids=true | all-gather | bytes 1280 | tf_op jit(solution)/shard_map/all_gather | solution.py:38
  341.9 22.6 %all-gather.17.cloned.1.call-done = bf16[4,2048,128]{2,1,0:T(8,128)(2,1)} async-done(((bf16[1,2048,128]{2,1,0:T(8,128)(2,1)}), bf16[4,2048,128]{2,1,0:T(8,128)(2,1)}) %all-gather.17.cloned.1.call-update) | async-done | bytes 2097168 | tf_op jit(solution)/shard_map/all_gather | solution.py:38
  364.5 3.9 fusion.313
  368.6 4.6 %all-gather.8 = bf16[2,1,128]{2,1,0:T(2,128)(2,1)S(1)} all-gather(bf16[1,1,128]{2,1,0:T(2,128)(2,1)S(1)} %get-tuple-element.218), channel_id=4, replica_groups=mesh['tm_0'=4,'tm_1'=2,'docs'=16] {'tm_1'}, dimensions={0}, use_global_device_ids=true | all-gather | bytes 768 | tf_op jit(solution)/shard_map/all_gather | solution.py:59
  373.2 20.7 %all-gather.23.cloned.1.call-done = bf16[4096,128]{1,0:T(8,128)(2,1)} async-done(((bf16[2048,128]{1,0:T(8,128)(2,1)}), bf16[4096,128]{1,0:T(8,128)(2,1)}) %all-gather.23.cloned.1.call-update) | async-done | bytes 1048592 | tf_op jit(solution)/shard_map/all_gather | solution.py:59
  393.8 2.2 fusion.37
  396.1 7.9 %all-gather.9 = bf16[4,1,128]{2,1,0:T(2,128)(2,1)S(1)} all-gather(bf16[1,1,128]{2,1,0:T(2,128)(2,1)S(1)} %get-tuple-element.212), channel_id=1, replica_groups=mesh['tm_0'=4,'tm_1'=2,'docs'=16] {'tm_0'}, dimensions={0}, use_global_device_ids=true | all-gather | bytes 1280 | tf_op jit(solution)/shard_map/all_gather | solution.py:59
  404.0 22.7 %all-gather.19.cloned.1.call-done = bf16[4,2048,128]{2,1,0:T(8,128)(2,1)} async-done(((bf16[1,2048,128]{2,1,0:T(8,128)(2,1)}), bf16[4,2048,128]{2,1,0:T(8,128)(2,1)}) %all-gather.19.cloned.1.call-update) | async-done | bytes 2097168 | tf_op jit(solution)/shard_map/all_gather | solution.py:59
  426.7 3.7 fusion.24
  (89 shorter events, 11.8 us)
Async XLA Ops:
  7.2 296.3 %reduce-scatter.2.cloned.1.call-start = ((), (), s32[]{:S(2)}) async-start(), calls=%async_computation.2 | async-start | bytes 8912896 | tf_op jit(solution)/shard_map/reduce_scatter | solution.py:124
  51.4 97.5 %copy-start.2 = (f32[128]{0:T(128)S(1)}, f32[128]{0:T(128)}, u32[]{:S(2)}) copy-start(f32[128]{0:T(128)} %param.13) | copy-start | bytes 1540
  51.4 97.5 %copy-start.5 = (f32[1,64,128]{2,1,0:T(8,128)S(1)}, f32[1,64,128]{2,1,0:T(8,128)}, u32[]{:S(2)}) copy-start(f32[1,64,128]{2,1,0:T(8,128)} %param.12) | copy-start | bytes 98308
  196.2 1.9 copy-start
  205.4 0.7 copy-start.1
  205.4 126.3 %all-gather.21.cloned.1.call-start = ((), (), s32[]{:S(2)}) async-start(), calls=%async_computation.5 | async-start | bytes 1572864 | tf_op jit(solution)/shard_map/all_gather | solution.py:38
  206.1 74.1 %copy-start.3 = (f32[128]{0:T(128)S(1)}, f32[128]{0:T(128)}, u32[]{:S(2)}) copy-start(f32[128]{0:T(128)} %param.15) | copy-start | bytes 1540
  206.1 75.0 %copy-start.4 = (pred[8]{0:T(512)(128)(4,1)S(1)}, pred[8]{0:T(512)(128)(4,1)}, u32[]{:S(2)}) copy-start(pred[8]{0:T(512)(128)(4,1)} %constant.117.clone.1) | copy-start | bytes 28
  305.5 59.0 %all-gather.17.cloned.1.call-start = ((), (), s32[]{:S(2)}) async-start(), calls=%async_computation.3 | async-start | bytes 2621440 | tf_op jit(solution)/shard_map/all_gather | solution.py:38
  333.9 59.9 %all-gather.23.cloned.1.call-start = ((), (), s32[]{:S(2)}) async-start(), calls=%async_computation.6 | async-start | bytes 1572864 | tf_op jit(solution)/shard_map/all_gather | solution.py:59
  368.5 58.1 %all-gather.19.cloned.1.call-start = ((), (), s32[]{:S(2)}) async-start(), calls=%async_computation.4 | async-start | bytes 2621440 | tf_op jit(solution)/shard_map/all_gather | solution.py:59
Sparse Core Ops, SparseCore 0:
  205.6 97.8 reduce-scatter.1
  305.7 26.0 all-gather.20
  334.1 30.4 all-gather.16
  368.6 25.1 all-gather.22
  396.2 30.4 all-gather.18
